TPU v7x, 32 devices: a whole 2x2x4 slice. The times are simulated.
32 devices in a mesh: gx: 4 (over z), gy: 4 (over y, core), gz: 2 (over x).
Axes of the slice: x: 2, y: 2, z: 4, core: 2. Of those that a mesh axis runs over, the one named last changes fastest.
Arguments:
- positions: float32 [4, 4, 2, 3, 32, 128], P('gx', 'gy', 'gz'), may hold values from 0 to 1
- velocities: float32 [4, 4, 2, 3, 32, 128], P('gx', 'gy', 'gz'), may hold values from -6 to 6
- strength: float32 [4, 4, 2, 32, 128], P('gx', 'gy', 'gz'), may hold values from 0.5 to 2
- tower_slots: int32 [4, 4, 2, 128], P('gx', 'gy', 'gz'), may hold values from 0 to 159
- plate_slots: int32 [4, 4, 2, 128], P('gx', 'gy', 'gz'), may hold values from 0 to 191
- pair_count: int32 [4, 4, 2], P('gx', 'gy', 'gz'), may hold values from 16 to 128, as said below
Outputs:
- new_positions: float32 [4, 4, 2, 3, 32, 128], P('gx', 'gy', 'gz')
- new_velocities: float32 [4, 4, 2, 3, 32, 128], P('gx', 'gy', 'gz')
Inputs may be any that keep to these rules, and one draw needn't show every extreme that they name: `pair_count`: slots at or beyond a device's count are padding. Some device has all 128 slots in use.
All inputs are finite; a program needn't handle non-finite values.
Results may differ from a plain program's by a relative error of at most 0.0003.
Values sent between devices are 32-bit elements; how exact they have to be, the bound alone decides.
No kernel may reach another device: no remote copies, remote signals or barrier semaphores. Data moves between devices by JAX's collectives and lax.ppermute only.
A program may use at most 64 MiB of HBM per device.

v0:
```python
import functools

import jax
import jax.numpy as jnp
from jax import lax
from jax.experimental import pallas as pl
from jax.experimental.pallas import tpu as pltpu
from jax.sharding import PartitionSpec as P


time_step = 0.02
repulsion = 4.0
reach = 2
lines = 3
group = 64
lead = 8
planes = 24
grant = 32 << 20


def split(value):
    high = value.astype(jnp.bfloat16).astype(jnp.float32)
    return high, value - high


def split_three(value):
    high, rest = split(value)
    middle, low = split(rest)
    return high, middle, low


def norm_of(place):
    return place[0] * place[0] + place[1] * place[1] + place[2] * place[2]


def write_planes(planes_ref, base, rows, clusters):
    for at, row in enumerate(rows):
        planes_ref[pl.ds(base + at * (clusters + 1), clusters), :] = row


def charges(place, strength):
    parts = [split(strength * value) for value in place] + [split(strength)]
    return [part[0] for part in parts] + [part[1] for part in parts]


def tower_rows(place, strength):
    ones = jnp.ones_like(strength)
    parts = [split(value) for value in place]
    high = [part[0] for part in parts]
    middle = [part[1] for part in parts]
    norm = split_three(-0.25 * norm_of(place))
    operand = high + [norm[0]] + high + [norm[1]] + middle + [norm[2], ones, ones, ones, 0.0 * ones]
    return operand + charges(place, strength)


def plate_rows(place, strength):
    ones = jnp.ones_like(strength)
    parts = [split(0.5 * value) for value in place]
    high = [part[0] for part in parts]
    middle = [part[1] for part in parts]
    norm = split_three(1.0 - 0.25 * norm_of(place))
    operand = high + [ones] + middle + [ones] + high + [ones] + list(norm) + [0.0 * ones]
    return operand + charges(place, strength)


def apply_sums(sums, base, place, strength, clusters):
    row = [sums[pl.ds(base + at * (clusters + 1), clusters), :] for at in range(8)]
    total = [row[at] + row[at + 4] for at in range(4)]
    scale = repulsion * strength
    return [scale * (place[at] * total[3] - total[at]) for at in range(3)]


def views(refs, where):
    return [
        refs[operand] if part is None else refs[operand].at[part] for operand, part in where
    ]


def pair_kernel(*refs, rows_held, lines_held, heights, clusters, where_place, where_strength):
    height_ref, count_ref, tower_list, plate_list = refs[:4]
    place_count = 1 + max(operand for operand, part in where_place)
    strength_count = 1 + max(operand for operand, part in where_strength)
    place_refs = views(refs[4 : 4 + place_count], where_place)
    strength_refs = views(refs[4 + place_count : 4 + place_count + strength_count], where_strength)
    force_refs = refs[4 + place_count + strength_count : -5]
    tower_planes, plate_planes, tower_sums, plate_sums, softs = refs[-5:]
    count = count_ref[0]
    height = height_ref[0]
    own_row = reach % rows_held
    towers = 2 * reach + 1
    pitch = clusters + 1
    blank_rows = jnp.zeros((8, tower_planes.shape[1]), jnp.float32)

    def tower_place(block):
        ref = place_refs[block % rows_held]
        return [ref[0] + (block - reach - 0.5), ref[1] - 1.0, ref[2] - 0.5]

    def plate_slot(line, rise):
        level = height + rise
        level = jnp.where(level >= heights, level - heights, level)
        return line * heights + level, (level - height).astype(jnp.float32) - 0.5

    def plate_place(line, rise, above):
        ref = place_refs[rows_held + line % lines_held * heights + rise]
        return [ref[0] - 0.5, ref[1] + (line - 1.0), ref[2] + above]

    for block in range(towers):
        strength = strength_refs[block % rows_held][3]
        base = block * (planes * pitch)
        write_planes(tower_planes, base, tower_rows(tower_place(block), strength), clusters)
    for line in range(lines):
        for rise in range(heights):
            slot, above = plate_slot(line, rise)
            strength = strength_refs[rows_held + line % lines_held * heights + rise][3]
            base = slot * (planes * pitch)
            rows = plate_rows(plate_place(line, rise, above), strength)
            write_planes(plate_planes, base, rows, clusters)
    for ref, sums, blocks_here in (
        (tower_planes, tower_sums, towers),
        (plate_planes, plate_sums, lines * heights),
    ):
        for at in range(0, planes, 8):
            ref[pl.ds(blocks_here * planes * pitch + at * pitch, 8, stride=pitch), :] = blank_rows
        for block in range(blocks_here + 1):
            sums[pl.ds(block * planes * pitch, 8 * pitch), :] = jnp.zeros(
                (8 * pitch, sums.shape[1]), jnp.float32
            )

    def operand_of(planes_ref, base):
        lower = planes_ref[pl.ds(base, 8, stride=pitch), :]
        upper = planes_ref[pl.ds(base + 8 * pitch, 8, stride=pitch), :]
        return jnp.concatenate([lower, upper], axis=0).astype(jnp.bfloat16)

    def charge_of(planes_ref, base):
        charge = planes_ref[pl.ds(base + 16 * pitch, 8, stride=pitch), :].astype(jnp.bfloat16)
        return jnp.concatenate([charge, charge], axis=1)

    def soft_of(begin):
        left = []
        right = []
        for side in range(2):
            operand_q = operand_of(plate_planes, plate_list[begin + side])
            blank = jnp.zeros_like(operand_q)
            left.append(operand_of(tower_planes, tower_list[begin + side]))
            pair = [operand_q, blank] if side == 0 else [blank, operand_q]
            right.append(jnp.concatenate(pair, axis=1))
        return lax.dot_general(
            jnp.concatenate(left, axis=0),
            jnp.concatenate(right, axis=0),
            (((0,), (0,)), ((), ())),
            preferred_element_type=jnp.float32,
        )

    def keep(soft, at):
        softs[at] = soft[:, : soft.shape[1] // 2]
        softs[at + 1] = soft[:, soft.shape[1] // 2 :]

    def consume(begin, ats):
        for at in ats:
            tower_base = tower_list[begin + at]
            plate_base = plate_list[begin + at]
            soft = jnp.maximum(softs[at % lead], 0.0)
            square = soft * soft
            high = square.astype(jnp.bfloat16)
            low = (square - high.astype(jnp.float32)).astype(jnp.bfloat16)
            on_plate = jnp.dot(
                charge_of(tower_planes, tower_base),
                jnp.concatenate([high, low], axis=0),
                preferred_element_type=jnp.float32,
            )
            on_tower = lax.dot_general(
                jnp.concatenate([high, low], axis=1),
                charge_of(plate_planes, plate_base),
                (((1,), (1,)), ((), ())),
                preferred_element_type=jnp.float32,
            ).T
            tower_at = pl.ds(tower_base, 8, stride=pitch)
            plate_at = pl.ds(plate_base, 8, stride=pitch)
            tower_sums[tower_at, :] = tower_sums[tower_at, :] + on_tower
            plate_sums[plate_at, :] = plate_sums[plate_at, :] + on_plate

    def advance(step, unused):
        begin = step * group
        for at in range(0, group, 2):
            following = soft_of(begin + lead + at)
            consume(begin, (at, at + 1))
            keep(following, at % lead)
        return unused

    for at in range(0, lead, 2):
        keep(soft_of(at), at)
    lax.fori_loop(0, lax.div(count + (group - 1), group), advance, 0)

    def tower_part(block):
        strength = strength_refs[block % rows_held][3]
        base = block * (planes * pitch)
        return apply_sums(tower_sums, base, tower_place(block), strength, clusters)

    def plate_part(line, rise):
        slot, above = plate_slot(line, rise)
        strength = strength_refs[rows_held + line % lines_held * heights + rise][3]
        base = slot * (planes * pitch)
        return apply_sums(plate_sums, base, plate_place(line, rise, above), strength, clusters)

    def add(first, second):
        return [one + two for one, two in zip(first, second)]

    forces = {}
    for block in range(towers):
        place = block % rows_held
        part = tower_part(block)
        forces[place] = add(forces[place], part) if place in forces else part
    for line in range(lines):
        for rise in range(heights):
            place = rows_held + line % lines_held * heights + rise
            part = plate_part(line, rise)
            forces[place] = add(forces[place], part) if place in forces else part
    forces[own_row] = add(forces[own_row], forces.pop(rows_held))
    targets = [(ref, held) for held, ref in enumerate(force_refs[:rows_held])]
    for line in range(1, lines_held):
        targets.append((force_refs[rows_held + line - 1], rows_held + line * heights))
    for rise in range(1, heights):
        ref = force_refs[rows_held + lines_held - 2 + rise]
        for line in range(lines_held):
            targets.append((ref.at[line], rows_held + line * heights + rise))
    for ref, held in targets:
        for at in range(3):
            ref[at] = forces[held][at]


def pair_forces(height, count, tower_list, plate_list, places, strengths, held, heights):
    rows_held, lines_held = held
    place_operands, where_place = places
    strength_operands, where_strength = strengths
    clusters, size = place_operands[0].shape[1:]
    towers = 2 * reach + 1
    kernel = functools.partial(
        pair_kernel,
        rows_held=rows_held,
        lines_held=lines_held,
        heights=heights,
        clusters=clusters,
        where_place=where_place,
        where_strength=where_strength,
    )
    smem = pl.BlockSpec(memory_space=pltpu.SMEM)
    vmem = pl.BlockSpec(memory_space=pltpu.VMEM)
    pairs = tower_list.shape[0]
    block_rows = planes * (clusters + 1)
    force = jax.ShapeDtypeStruct((3, clusters, size), jnp.float32)
    raised = jax.ShapeDtypeStruct((lines_held, 3, clusters, size), jnp.float32)
    out_shape = (force,) * (rows_held + lines_held - 1) + (raised,) * (heights - 1)
    return pl.pallas_call(
        kernel,
        out_shape=out_shape,
        in_specs=[smem] * 4 + [vmem] * (len(place_operands) + len(strength_operands)),
        out_specs=(vmem,) * len(out_shape),
        scratch_shapes=[
            pltpu.VMEM(((towers + 1) * block_rows, size), jnp.float32),
            pltpu.VMEM(((lines * heights + 1) * block_rows, size), jnp.float32),
            pltpu.VMEM(((towers + 1) * block_rows, size), jnp.float32),
            pltpu.VMEM(((lines * heights + 1) * block_rows, size), jnp.float32),
            pltpu.VMEM((lead, size, size), jnp.float32),
        ],
        compiler_params=pltpu.CompilerParams(vmem_limit_bytes=grant),
        cost_estimate=pl.CostEstimate(
            flops=pairs * size * size * 40, bytes_accessed=1 << 20, transcendentals=0
        ),
    )(height, count, tower_list, plate_list, *place_operands, *strength_operands)


def shift_row(value, steps, count):
    return lax.ppermute(value, "gx", [(at, (at + steps) % count) for at in range(count)])


def shift_plane(value, line_steps, height_steps, line_count, height_count):
    pairs = [
        (
            at * height_count + up,
            (at + line_steps) % line_count * height_count + (up + height_steps) % height_count,
        )
        for at in range(line_count)
        for up in range(height_count)
    ]
    return lax.ppermute(value, ("gy", "gz"), pairs)


def plan(row_count, line_count, height_count):
    rows_held = min(row_count, 2 * reach + 1)
    lines_held = min(line_count, lines)
    rows = [(held - reach) % row_count for held in range(rows_held)]
    plates = [(line, rise) for line in range(lines_held) for rise in range(height_count)]
    return rows, plates, lines_held


def issue_order(rows, plates):
    far_rows = sorted((offset for offset in rows if offset != 0), reverse=True)
    near = sorted((place for place in plates if place != (0, 0)), key=lambda at: (-at[1], -at[0]))
    return far_rows + near


def collect(value, rows, plates, sizes):
    row_count, line_count, height_count = sizes
    got = {}
    issued = issue_order(rows, plates)[::-1]
    for place in issued:
        if isinstance(place, tuple):
            line, rise = place
            got[place] = shift_plane(value, -line, -rise, line_count, height_count)
        else:
            got[place] = shift_row(value, -place, row_count)
    got[0] = value
    operands = [0] + issued
    where = [(operands.index(key), None) for key in rows]
    where += [(operands.index(key if key != (0, 0) else 0), None) for key in plates]
    return [got[key] for key in operands], tuple(where)


def far_rows(rows):
    return sorted((offset for offset in rows if offset != 0), reverse=True)


def collect_again(value, rows, lines_held, sizes):
    row_count, line_count, height_count = sizes
    operands = [value]
    where_line = [0]
    for line in range(lines_held - 1, 0, -1):
        operands.append(shift_plane(value, -line, 0, line_count, height_count))
    where_line += list(range(lines_held - 1, 0, -1))
    where_row = {0: 0}
    for offset in far_rows(rows):
        operands.append(shift_row(value, -offset, row_count))
        where_row[offset] = len(operands) - 1
    column = jnp.stack([operands[at] for at in where_line])
    where_rise = {}
    for rise in range(1, height_count):
        operands.append(shift_plane(column, 0, -rise, line_count, height_count))
        where_rise[rise] = len(operands) - 1
    where = [(where_row[offset], None) for offset in rows]
    for line in range(lines_held):
        where.append((where_line[line], None))
        where += [(where_rise[rise], line) for rise in range(1, height_count)]
    return operands, tuple(where)


def give_back(forces, rows, lines_held, sizes):
    row_count, line_count, height_count = sizes
    remote = dict(zip(rows, forces))
    total = remote.pop(0)
    own_lines = list(forces[len(rows) : len(rows) + lines_held - 1])
    raised = forces[len(rows) + lines_held - 1 :]
    moved = []
    for rise in range(1, height_count):
        moved.append(shift_plane(raised[rise - 1], 0, rise, line_count, height_count))
    for part in moved:
        own_lines = [own + part[at + 1] for at, own in enumerate(own_lines)]
        total = total + part[0]
    came = []
    for offset in far_rows(rows):
        came.append(shift_row(remote[offset], offset, row_count))
    for line in range(lines_held - 1, 0, -1):
        came.append(shift_plane(own_lines[line - 1], line, 0, line_count, height_count))
    for part in came:
        total = total + part
    return total


def bases_of(slots, count, clusters, blank_block):
    block_rows = planes * (clusters + 1)
    base = lax.div(slots, clusters) * block_rows + lax.rem(slots, clusters)
    live = lax.broadcasted_iota(jnp.int32, slots.shape, 0) < count
    base = jnp.where(live, base, blank_block * block_rows)
    return jnp.pad(base, (0, group + lead), constant_values=blank_block * block_rows)


def shards(positions, velocities, strength, tower_slots, plate_slots, pair_count):
    coords = positions[0, 0, 0]
    speeds = velocities[0, 0, 0]
    tower_list = tower_slots[0, 0, 0]
    plate_list = plate_slots[0, 0, 0]
    count = pair_count.reshape(1)
    clusters = coords.shape[1]
    sizes = tuple(lax.axis_size(name) for name in ("gx", "gy", "gz"))
    tower_list = bases_of(tower_list, count[0], clusters, 2 * reach + 1)
    plate_list = bases_of(plate_list, count[0], clusters, lines * sizes[2])
    rows, plates, lines_held = plan(*sizes)
    height = lax.axis_index("gz").astype(jnp.int32).reshape(1)
    packed = jnp.concatenate([coords, strength[0, 0]], axis=0)
    strengths = collect(packed, rows, plates, sizes)
    places = strengths
    for leap_index in range(2):
        if leap_index > 0:
            places = collect_again(coords, rows, lines_held, sizes)
        forces = pair_forces(
            height,
            count,
            tower_list,
            plate_list,
            places,
            strengths,
            (len(rows), lines_held),
            sizes[2],
        )
        force = give_back(forces, rows, lines_held, sizes)
        speeds = speeds + time_step * force
        coords = coords + time_step * speeds
    return (coords[None, None, None], speeds[None, None, None])


def solution(mesh):
    in_specs = (
        P("gx", "gy", "gz", None, None, None),
        P("gx", "gy", "gz", None, None, None),
        P("gx", "gy", "gz", None, None),
        P("gx", "gy", "gz", None),
        P("gx", "gy", "gz", None),
        P("gx", "gy", "gz"),
    )
    out_specs = (P("gx", "gy", "gz", None, None, None), P("gx", "gy", "gz", None, None, None))
    return jax.shard_map(
        shards, mesh=mesh, in_specs=in_specs, out_specs=out_specs, check_vma=False
    )
```

profile of v0, /device:TPU:0, one launch (start us, length us, event | category | flops | bytes accessed | tf_op | source)
XLA Modules:
  0.0 61.0 jit_solution(6338997189056792770)
XLA Ops:
  0.6 0.8 %pad_maximum_fusion.1.refs_4_.refs_13_.refs_11_ = f32[4,32,128]{2,1,0:T(8,128)S(1)} fusion(f32[1,32,128]{2,1,0:T(8,128)} %bitcast.97, f32[3,32,128]{2,1,0:T(8,128)} %bitcast.95), kind=kLoop, calls=%fused_computation.1 | loop fusion | flops 16384 | bytes 131072 | tf_op jit(solution)/shard_map/concatenate | solution.py:388
  1.5 3.1 %collective-permute-start.7 = (f32[4,32,128]{2,1,0:T(8,128)S(1)}, f32[4,32,128]{2,1,0:T(8,128)S(1)}, u32[]{:S(2)}, u32[]{:S(2)}) collective-permute-start(f32[4,32,128]{2,1,0:T(8,128)S(1)} %pad_maximum_fusion.1.refs_4_.refs_13_.refs_11_), channel_id=1, source_target_pairs={{0,8},{8,16},{16,24},{24,0},{1,9},{9,17},{17,25},{25,1},{2,10},{10... | collective-permute-start | bytes 196616 | tf_op jit(solution)/shard_map/ppermute | solution.py:273
  4.5 2.6 %collective-permute-start.6 = (f32[4,32,128]{2,1,0:T(8,128)S(1)}, f32[4,32,128]{2,1,0:T(8,128)S(1)}, u32[]{:S(2)}, u32[]{:S(2)}) collective-permute-start(f32[4,32,128]{2,1,0:T(8,128)S(1)} %pad_maximum_fusion.1.refs_4_.refs_13_.refs_11_), channel_id=1, source_target_pairs={{0,16},{8,24},{16,0},{24,8},{1,17},{9,25},{17,1},{25,9},{2,18},{10... | collective-permute-start | bytes 196616 | tf_op jit(solution)/shard_map/ppermute | solution.py:273
  7.1 1.3 %collective-permute-start.5 = (f32[4,32,128]{2,1,0:T(8,128)S(1)}, f32[4,32,128]{2,1,0:T(8,128)S(1)}, u32[]{:S(2)}, u32[]{:S(2)}) collective-permute-start(f32[4,32,128]{2,1,0:T(8,128)S(1)} %pad_maximum_fusion.1.refs_4_.refs_13_.refs_11_), channel_id=1, source_target_pairs={{0,24},{8,0},{16,8},{24,16},{1,25},{9,1},{17,9},{25,17},{2,26},{10... | collective-permute-start | bytes 196616 | tf_op jit(solution)/shard_map/ppermute | solution.py:273
  8.4 2.4 %collective-permute-start.4 = (f32[4,32,128]{2,1,0:T(8,128)S(1)}, f32[4,32,128]{2,1,0:T(8,128)S(1)}, u32[]{:S(2)}, u32[]{:S(2)}) collective-permute-start(f32[4,32,128]{2,1,0:T(8,128)S(1)} %pad_maximum_fusion.1.refs_4_.refs_13_.refs_11_), channel_id=1, source_target_pairs={{0,5},{1,4},{2,7},{3,6},{4,1},{5,0},{6,3},{7,2},{8,13},{9,12},{10,... | collective-permute-start | bytes 196616 | tf_op jit(solution)/shard_map/ppermute | solution.py:285
  12.2 1.3 %collective-permute-start.1 = (f32[4,32,128]{2,1,0:T(8,128)S(1)}, f32[4,32,128]{2,1,0:T(8,128)S(1)}, u32[]{:S(2)}, u32[]{:S(2)}) collective-permute-start(f32[4,32,128]{2,1,0:T(8,128)S(1)} %pad_maximum_fusion.1.refs_4_.refs_13_.refs_11_), channel_id=1, source_target_pairs={{0,4},{1,5},{2,6},{3,7},{4,0},{5,1},{6,2},{7,3},{8,12},{9,13},{10,... | collective-permute-start | bytes 196616 | tf_op jit(solution)/shard_map/ppermute | solution.py:285
  13.5 1.4 %collective-permute-start = (f32[4,32,128]{2,1,0:T(8,128)S(1)}, f32[4,32,128]{2,1,0:T(8,128)S(1)}, u32[]{:S(2)}, u32[]{:S(2)}) collective-permute-start(f32[4,32,128]{2,1,0:T(8,128)S(1)} %pad_maximum_fusion.1.refs_4_.refs_13_.refs_11_), channel_id=1, source_target_pairs={{0,6},{1,7},{2,0},{3,1},{4,2},{5,3},{6,4},{7,5},{8,14},{9,15},{10,... | collective-permute-start | bytes 196616 | tf_op jit(solution)/shard_map/ppermute | solution.py:285
  15.1 1.4 %collective-permute-done.2.refs_7_.refs_16_.refs_14_ = f32[4,32,128]{2,1,0:T(8,128)S(1)} collective-permute-done((f32[4,32,128]{2,1,0:T(8,128)S(1)}, f32[4,32,128]{2,1,0:T(8,128)S(1)}, u32[]{:S(2)}, u32[]{:S(2)}) %collective-permute-start.2) | collective-permute-done | bytes 65568 | tf_op jit(solution)/shard_map/ppermute | solution.py:285
  16.8 3.3 %shard_map.77 = (f32[3,32,128]{2,1,0:T(8,128)S(1)}, f32[3,32,128]{2,1,0:T(8,128)S(1)}, f32[3,32,128]{2,1,0:T(8,128)S(1)}, f32[3,32,128]{2,1,0:T(8,128)S(1)}, f32...) custom-call(s32[1]{0:T(128)} %bitcast.2.refs_0_, s32[1]{0:T(128)} %bitcast.89.refs_1_, ...), custom_call_target="tpu_custom_call" | custom-call | flops 131072000 | bytes 1048576 | tf_op jit(solution)/shard_map/pallas_call | solution.py:253
  20.1 1.4 %collective-permute-start.8 = (f32[3,3,32,128]{3,2,1,0:T(8,128)S(1)}, f32[3,3,32,128]{3,2,1,0:T(8,128)S(1)}, u32[]{:S(2)}, u32[]{:S(2)}) collective-permute-start(f32[3,3,32,128]{3,2,1,0:T(8,128)S(1)} %get-tuple-element.17), channel_id=1, source_target_pairs={{0,1},{1,0},{2,3},{3,2},{4,5},{5,4},{6,7},{7,6},{8,9},{9,8},{10,11... | collective-permute-start | bytes 442376 | tf_op jit(solution)/shard_map/ppermute | solution.py:285
  21.5 2.5 %collective-permute-start.9 = (f32[3,32,128]{2,1,0:T(8,128)S(1)}, f32[3,32,128]{2,1,0:T(8,128)S(1)}, u32[]{:S(2)}, u32[]{:S(2)}) collective-permute-start(f32[3,32,128]{2,1,0:T(8,128)S(1)} %get-tuple-element.18), channel_id=1, source_target_pairs={{0,24},{8,0},{16,8},{24,16},{1,25},{9,1},{17,9},{25,17},{2,26},{10... | collective-permute-start | bytes 147464 | tf_op jit(solution)/shard_map/ppermute | solution.py:273
  24.5 0.8 %collective-permute-done.8 = f32[3,3,32,128]{3,2,1,0:T(8,128)S(1)} collective-permute-done((f32[3,3,32,128]{3,2,1,0:T(8,128)S(1)}, f32[3,3,32,128]{3,2,1,0:T(8,128)S(1)}, u32[]{:S(2)}, u32[]{:S(2)}) %collective-permute-start.8) | collective-permute-done | bytes 147488 | tf_op jit(solution)/shard_map/ppermute | solution.py:285
  25.4 2.8 %collective-permute-start.12 = (f32[3,32,128]{2,1,0:T(8,128)S(1)}, f32[3,32,128]{2,1,0:T(8,128)S(1)}, u32[]{:S(2)}, u32[]{:S(2)}) collective-permute-start(f32[3,32,128]{2,1,0:T(8,128)S(1)} %get-tuple-element.36), channel_id=1, source_target_pairs={{0,4},{1,5},{2,6},{3,7},{4,0},{5,1},{6,2},{7,3},{8,12},{9,13},{10,... | collective-permute-start | bytes 147464 | tf_op jit(solution)/shard_map/ppermute | solution.py:285
  28.2 2.3 %collective-permute-done.10 = f32[3,32,128]{2,1,0:T(8,128)S(1)} collective-permute-done((f32[3,32,128]{2,1,0:T(8,128)S(1)}, f32[3,32,128]{2,1,0:T(8,128)S(1)}, u32[]{:S(2)}, u32[]{:S(2)}) %collective-permute-start.10) | collective-permute-done | bytes 49184 | tf_op jit(solution)/shard_map/ppermute | solution.py:273
  30.8 0.9 %collective-permute-done.13 = f32[3,32,128]{2,1,0:T(8,128)S(1)} collective-permute-done((f32[3,32,128]{2,1,0:T(8,128)S(1)}, f32[3,32,128]{2,1,0:T(8,128)S(1)}, u32[]{:S(2)}, u32[]{:S(2)}) %collective-permute-start.13) | collective-permute-done | bytes 49184 | tf_op jit(solution)/shard_map/ppermute | solution.py:285
  32.6 1.5 %collective-permute-done.15.refs_6_ = f32[3,32,128]{2,1,0:T(8,128)S(1)} collective-permute-done((f32[3,32,128]{2,1,0:T(8,128)S(1)}, f32[3,32,128]{2,1,0:T(8,128)S(1)}, u32[]{:S(2)}, u32[]{:S(2)}) %collective-permute-start.15) | collective-permute-done | bytes 49184 | tf_op jit(solution)/shard_map/ppermute | solution.py:285
  34.1 2.3 %collective-permute-done.14.refs_5_ = f32[3,32,128]{2,1,0:T(8,128)S(1)} collective-permute-done((f32[3,32,128]{2,1,0:T(8,128)S(1)}, f32[3,32,128]{2,1,0:T(8,128)S(1)}, u32[]{:S(2)}, u32[]{:S(2)}) %collective-permute-start.14) | collective-permute-done | bytes 49184 | tf_op jit(solution)/shard_map/ppermute | solution.py:285
  36.4 1.4 %collective-permute-start.19 = (f32[3,3,32,128]{3,2,1,0:T(8,128)S(1)}, f32[3,3,32,128]{3,2,1,0:T(8,128)S(1)}, u32[]{:S(2)}, u32[]{:S(2)}) collective-permute-start(f32[3,3,32,128]{3,2,1,0:T(8,128)S(1)} %pad_maximum_fusion), channel_id=1, source_target_pairs={{0,1},{1,0},{2,3},{3,2},{4,5},{5,4},{6,7},{7,6},{8,9},{9,8},{10,11... | collective-permute-start | bytes 442376 | tf_op jit(solution)/shard_map/ppermute | solution.py:285
  37.8 2.2 %collective-permute-start.18 = (f32[3,32,128]{2,1,0:T(8,128)S(1)}, f32[3,32,128]{2,1,0:T(8,128)S(1)}, u32[]{:S(2)}, u32[]{:S(2)}) collective-permute-start(f32[3,32,128]{2,1,0:T(8,128)S(1)} %get-tuple-element.32.refs_4_), channel_id=1, source_target_pairs={{0,24},{8,0},{16,8},{24,16},{1,25},{9,1},{17,9},{25,17},{2,26},{10... | collective-permute-start | bytes 147464 | tf_op jit(solution)/shard_map/ppermute | solution.py:273
  40.0 0.8 %collective-permute-start.16 = (f32[3,32,128]{2,1,0:T(8,128)S(1)}, f32[3,32,128]{2,1,0:T(8,128)S(1)}, u32[]{:S(2)}, u32[]{:S(2)}) collective-permute-start(f32[3,32,128]{2,1,0:T(8,128)S(1)} %get-tuple-element.32.refs_4_), channel_id=1, source_target_pairs={{0,8},{8,16},{16,24},{24,0},{1,9},{9,17},{17,25},{25,1},{2,10},{10... | collective-permute-start | bytes 147464 | tf_op jit(solution)/shard_map/ppermute | solution.py:273
  40.8 1.1 %collective-permute-done.18.refs_9_ = f32[3,32,128]{2,1,0:T(8,128)S(1)} collective-permute-done((f32[3,32,128]{2,1,0:T(8,128)S(1)}, f32[3,32,128]{2,1,0:T(8,128)S(1)}, u32[]{:S(2)}, u32[]{:S(2)}) %collective-permute-start.18) | collective-permute-done | bytes 49184 | tf_op jit(solution)/shard_map/ppermute | solution.py:273
  41.9 3.1 %collective-permute-done.17.refs_8_ = f32[3,32,128]{2,1,0:T(8,128)S(1)} collective-permute-done((f32[3,32,128]{2,1,0:T(8,128)S(1)}, f32[3,32,128]{2,1,0:T(8,128)S(1)}, u32[]{:S(2)}, u32[]{:S(2)}) %collective-permute-start.17) | collective-permute-done | bytes 49184 | tf_op jit(solution)/shard_map/ppermute | solution.py:273
  45.0 0.9 %collective-permute-done.16.refs_7_ = f32[3,32,128]{2,1,0:T(8,128)S(1)} collective-permute-done((f32[3,32,128]{2,1,0:T(8,128)S(1)}, f32[3,32,128]{2,1,0:T(8,128)S(1)}, u32[]{:S(2)}, u32[]{:S(2)}) %collective-permute-start.16) | collective-permute-done | bytes 49184 | tf_op jit(solution)/shard_map/ppermute | solution.py:273
  45.9 3.3 %shard_map.78 = (f32[3,32,128]{2,1,0:T(8,128)S(1)}, f32[3,32,128]{2,1,0:T(8,128)S(1)}, f32[3,32,128]{2,1,0:T(8,128)S(1)}, f32[3,32,128]{2,1,0:T(8,128)S(1)}, f32...) custom-call(s32[1]{0:T(128)} %bitcast.2.refs_0_, s32[1]{0:T(128)} %bitcast.90.refs_1_, ...), custom_call_target="tpu_custom_call" | custom-call | flops 131072000 | bytes 1048576 | tf_op jit(solution)/shard_map/pallas_call | solution.py:253
  49.3 1.3 %collective-permute-start.20 = (f32[3,3,32,128]{3,2,1,0:T(8,128)S(1)}, f32[3,3,32,128]{3,2,1,0:T(8,128)S(1)}, u32[]{:S(2)}, u32[]{:S(2)}) collective-permute-start(f32[3,3,32,128]{3,2,1,0:T(8,128)S(1)} %get-tuple-element.24), channel_id=1, source_target_pairs={{0,1},{1,0},{2,3},{3,2},{4,5},{5,4},{6,7},{7,6},{8,9},{9,8},{10,11... | collective-permute-start | bytes 442376 | tf_op jit(solution)/shard_map/ppermute | solution.py:285
  51.0 1.9 %collective-permute-start.23 = (f32[3,32,128]{2,1,0:T(8,128)S(1)}, f32[3,32,128]{2,1,0:T(8,128)S(1)}, u32[]{:S(2)}, u32[]{:S(2)}) collective-permute-start(f32[3,32,128]{2,1,0:T(8,128)S(1)} %get-tuple-element.27), channel_id=1, source_target_pairs={{0,8},{8,16},{16,24},{24,0},{1,9},{9,17},{17,25},{25,1},{2,10},{10... | collective-permute-start | bytes 147464 | tf_op jit(solution)/shard_map/ppermute | solution.py:273
  52.9 1.7 %collective-permute-done.20 = f32[3,3,32,128]{3,2,1,0:T(8,128)S(1)} collective-permute-done((f32[3,3,32,128]{3,2,1,0:T(8,128)S(1)}, f32[3,3,32,128]{3,2,1,0:T(8,128)S(1)}, u32[]{:S(2)}, u32[]{:S(2)}) %collective-permute-start.20) | collective-permute-done | bytes 147488 | tf_op jit(solution)/shard_map/ppermute | solution.py:285
  54.6 2.3 %collective-permute-start.24 = (f32[3,32,128]{2,1,0:T(8,128)S(1)}, f32[3,32,128]{2,1,0:T(8,128)S(1)}, u32[]{:S(2)}, u32[]{:S(2)}) collective-permute-start(f32[3,32,128]{2,1,0:T(8,128)S(1)} %get-tuple-element.34), channel_id=1, source_target_pairs={{0,4},{1,5},{2,6},{3,7},{4,0},{5,1},{6,2},{7,3},{8,12},{9,13},{10,... | collective-permute-start | bytes 147464 | tf_op jit(solution)/shard_map/ppermute | solution.py:285
  56.8 0.7 %collective-permute-done.23 = f32[3,32,128]{2,1,0:T(8,128)S(1)} collective-permute-done((f32[3,32,128]{2,1,0:T(8,128)S(1)}, f32[3,32,128]{2,1,0:T(8,128)S(1)}, u32[]{:S(2)}, u32[]{:S(2)}) %collective-permute-start.23) | collective-permute-done | bytes 49184 | tf_op jit(solution)/shard_map/ppermute | solution.py:273
  57.5 1.4 %collective-permute-done.24 = f32[3,32,128]{2,1,0:T(8,128)S(1)} collective-permute-done((f32[3,32,128]{2,1,0:T(8,128)S(1)}, f32[3,32,128]{2,1,0:T(8,128)S(1)}, u32[]{:S(2)}, u32[]{:S(2)}) %collective-permute-start.24) | collective-permute-done | bytes 49184 | tf_op jit(solution)/shard_map/ppermute | solution.py:285
  58.9 1.4 %collective-permute-done.25 = f32[3,32,128]{2,1,0:T(8,128)S(1)} collective-permute-done((f32[3,32,128]{2,1,0:T(8,128)S(1)}, f32[3,32,128]{2,1,0:T(8,128)S(1)}, u32[]{:S(2)}, u32[]{:S(2)}) %collective-permute-start.25) | collective-permute-done | bytes 49184 | tf_op jit(solution)/shard_map/ppermute | solution.py:285
  60.3 0.7 %add_bitcast_fusion = (f32[1,1,1,3,32,128]{5,4,3,2,1,0:T(8,128)}, f32[3,32,128]{2,1,0:T(8,128)}) fusion(f32[3,32,128]{2,1,0:T(8,128)S(1)} %get-tuple-element.32.refs_4_, f32[3,32,128]{2,1,0:T(8,128)S(1)} %get-tuple-element.33, f32[3,32,128]{2,1,0:T(8,128)S(1)} %collective-permute-done.25, f32[3,32,128]{2,1,0:T(8,128)S(1)} %collective-permute-done.24, ...), kind=kLoop, calls=%fused_computation.28 | loop fusion | flops 122880 | bytes 540672 | tf_op jit(solution)/shard_map/broadcast_in_dim | solution.py:407
  (39 shorter events, 3.3 us)
Async XLA Ops:
  1.5 10.1 %collective-permute-start.7 = (f32[4,32,128]{2,1,0:T(8,128)S(1)}, f32[4,32,128]{2,1,0:T(8,128)S(1)}, u32[]{:S(2)}, u32[]{:S(2)}) collective-permute-start(f32[4,32,128]{2,1,0:T(8,128)S(1)} %pad_maximum_fusion.1.refs_4_.refs_13_.refs_11_), channel_id=1, source_target_pairs={{0,8},{8,16},{16,24},{24,0},{1,9},{9,17},{17,25},{25,1},{2,10},{10... | collective-permute-start | bytes 196616 | tf_op jit(solution)/shard_map/ppermute | solution.py:273
  4.5 7.7 %collective-permute-start.6 = (f32[4,32,128]{2,1,0:T(8,128)S(1)}, f32[4,32,128]{2,1,0:T(8,128)S(1)}, u32[]{:S(2)}, u32[]{:S(2)}) collective-permute-start(f32[4,32,128]{2,1,0:T(8,128)S(1)} %pad_maximum_fusion.1.refs_4_.refs_13_.refs_11_), channel_id=1, source_target_pairs={{0,16},{8,24},{16,0},{24,8},{1,17},{9,25},{17,1},{25,9},{2,18},{10... | collective-permute-start | bytes 196616 | tf_op jit(solution)/shard_map/ppermute | solution.py:273
  7.1 6.4 %collective-permute-start.5 = (f32[4,32,128]{2,1,0:T(8,128)S(1)}, f32[4,32,128]{2,1,0:T(8,128)S(1)}, u32[]{:S(2)}, u32[]{:S(2)}) collective-permute-start(f32[4,32,128]{2,1,0:T(8,128)S(1)} %pad_maximum_fusion.1.refs_4_.refs_13_.refs_11_), channel_id=1, source_target_pairs={{0,24},{8,0},{16,8},{24,16},{1,25},{9,1},{17,9},{25,17},{2,26},{10... | collective-permute-start | bytes 196616 | tf_op jit(solution)/shard_map/ppermute | solution.py:273
  8.4 6.5 %collective-permute-start.4 = (f32[4,32,128]{2,1,0:T(8,128)S(1)}, f32[4,32,128]{2,1,0:T(8,128)S(1)}, u32[]{:S(2)}, u32[]{:S(2)}) collective-permute-start(f32[4,32,128]{2,1,0:T(8,128)S(1)} %pad_maximum_fusion.1.refs_4_.refs_13_.refs_11_), channel_id=1, source_target_pairs={{0,5},{1,4},{2,7},{3,6},{4,1},{5,0},{6,3},{7,2},{8,13},{9,12},{10,... | collective-permute-start | bytes 196616 | tf_op jit(solution)/shard_map/ppermute | solution.py:285
  10.9 4.2 %collective-permute-start.3 = (f32[4,32,128]{2,1,0:T(8,128)S(1)}, f32[4,32,128]{2,1,0:T(8,128)S(1)}, u32[]{:S(2)}, u32[]{:S(2)}) collective-permute-start(f32[4,32,128]{2,1,0:T(8,128)S(1)} %pad_maximum_fusion.1.refs_4_.refs_13_.refs_11_), channel_id=1, source_target_pairs={{0,7},{1,6},{2,1},{3,0},{4,3},{5,2},{6,5},{7,4},{8,15},{9,14},{10,... | collective-permute-start | bytes 196616 | tf_op jit(solution)/shard_map/ppermute | solution.py:285
  11.5 3.3 %copy-start.2 = (s32[1,1,1,128]{3,2,1,0:T(1,128)S(1)}, s32[1,1,1,128]{3,2,1,0:T(1,128)}, u32[]{:S(2)}) copy-start(s32[1,1,1,128]{3,2,1,0:T(1,128)} %param.10) | copy-start | bytes 1540
  11.6 3.3 %copy-start.3 = (s32[1,1,1,128]{3,2,1,0:T(1,128)S(1)}, s32[1,1,1,128]{3,2,1,0:T(1,128)}, u32[]{:S(2)}) copy-start(s32[1,1,1,128]{3,2,1,0:T(1,128)} %param.9) | copy-start | bytes 1540
  11.6 4.9 %collective-permute-start.2 = (f32[4,32,128]{2,1,0:T(8,128)S(1)}, f32[4,32,128]{2,1,0:T(8,128)S(1)}, u32[]{:S(2)}, u32[]{:S(2)}) collective-permute-start(f32[4,32,128]{2,1,0:T(8,128)S(1)} %pad_maximum_fusion.1.refs_4_.refs_13_.refs_11_), channel_id=1, source_target_pairs={{0,1},{1,0},{2,3},{3,2},{4,5},{5,4},{6,7},{7,6},{8,9},{9,8},{10,11... | collective-permute-start | bytes 196616 | tf_op jit(solution)/shard_map/ppermute | solution.py:285
  12.2 4.6 %collective-permute-start.1 = (f32[4,32,128]{2,1,0:T(8,128)S(1)}, f32[4,32,128]{2,1,0:T(8,128)S(1)}, u32[]{:S(2)}, u32[]{:S(2)}) collective-permute-start(f32[4,32,128]{2,1,0:T(8,128)S(1)} %pad_maximum_fusion.1.refs_4_.refs_13_.refs_11_), channel_id=1, source_target_pairs={{0,4},{1,5},{2,6},{3,7},{4,0},{5,1},{6,2},{7,3},{8,12},{9,13},{10,... | collective-permute-start | bytes 196616 | tf_op jit(solution)/shard_map/ppermute | solution.py:285
  13.5 3.3 %collective-permute-start = (f32[4,32,128]{2,1,0:T(8,128)S(1)}, f32[4,32,128]{2,1,0:T(8,128)S(1)}, u32[]{:S(2)}, u32[]{:S(2)}) collective-permute-start(f32[4,32,128]{2,1,0:T(8,128)S(1)} %pad_maximum_fusion.1.refs_4_.refs_13_.refs_11_), channel_id=1, source_target_pairs={{0,6},{1,7},{2,0},{3,1},{4,2},{5,3},{6,4},{7,5},{8,14},{9,15},{10,... | collective-permute-start | bytes 196616 | tf_op jit(solution)/shard_map/ppermute | solution.py:285
  20.1 5.2 %collective-permute-start.8 = (f32[3,3,32,128]{3,2,1,0:T(8,128)S(1)}, f32[3,3,32,128]{3,2,1,0:T(8,128)S(1)}, u32[]{:S(2)}, u32[]{:S(2)}) collective-permute-start(f32[3,3,32,128]{3,2,1,0:T(8,128)S(1)} %get-tuple-element.17), channel_id=1, source_target_pairs={{0,1},{1,0},{2,3},{3,2},{4,5},{5,4},{6,7},{7,6},{8,9},{9,8},{10,11... | collective-permute-start | bytes 442376 | tf_op jit(solution)/shard_map/ppermute | solution.py:285
  21.5 6.7 %collective-permute-start.9 = (f32[3,32,128]{2,1,0:T(8,128)S(1)}, f32[3,32,128]{2,1,0:T(8,128)S(1)}, u32[]{:S(2)}, u32[]{:S(2)}) collective-permute-start(f32[3,32,128]{2,1,0:T(8,128)S(1)} %get-tuple-element.18), channel_id=1, source_target_pairs={{0,24},{8,0},{16,8},{24,16},{1,25},{9,1},{17,9},{25,17},{2,26},{10... | collective-permute-start | bytes 147464 | tf_op jit(solution)/shard_map/ppermute | solution.py:273
  24.0 6.6 %collective-permute-start.10 = (f32[3,32,128]{2,1,0:T(8,128)S(1)}, f32[3,32,128]{2,1,0:T(8,128)S(1)}, u32[]{:S(2)}, u32[]{:S(2)}) collective-permute-start(f32[3,32,128]{2,1,0:T(8,128)S(1)} %get-tuple-element.19), channel_id=1, source_target_pairs={{0,16},{8,24},{16,0},{24,8},{1,17},{9,25},{17,1},{25,9},{2,18},{10... | collective-permute-start | bytes 147464 | tf_op jit(solution)/shard_map/ppermute | solution.py:273
  24.0 6.6 %collective-permute-start.11 = (f32[3,32,128]{2,1,0:T(8,128)S(1)}, f32[3,32,128]{2,1,0:T(8,128)S(1)}, u32[]{:S(2)}, u32[]{:S(2)}) collective-permute-start(f32[3,32,128]{2,1,0:T(8,128)S(1)} %get-tuple-element.20), channel_id=1, source_target_pairs={{0,8},{8,16},{16,24},{24,0},{1,9},{9,17},{17,25},{25,1},{2,10},{10... | collective-permute-start | bytes 147464 | tf_op jit(solution)/shard_map/ppermute | solution.py:273
  25.3 6.4 %copy-start = (f32[1,1,1,3,32,128]{5,4,3,2,1,0:T(8,128)S(1)}, f32[1,1,1,3,32,128]{5,4,3,2,1,0:T(8,128)}, u32[]{:S(2)}) copy-start(f32[1,1,1,3,32,128]{5,4,3,2,1,0:T(8,128)} %param.6) | copy-start | bytes 147460
  25.3 6.4 %copy-start.1 = (f32[1,1,1,3,32,128]{5,4,3,2,1,0:T(8,128)S(1)}, f32[1,1,1,3,32,128]{5,4,3,2,1,0:T(8,128)}, u32[]{:S(2)}) copy-start(f32[1,1,1,3,32,128]{5,4,3,2,1,0:T(8,128)} %param.7) | copy-start | bytes 147460
  25.4 5.4 %collective-permute-start.12 = (f32[3,32,128]{2,1,0:T(8,128)S(1)}, f32[3,32,128]{2,1,0:T(8,128)S(1)}, u32[]{:S(2)}, u32[]{:S(2)}) collective-permute-start(f32[3,32,128]{2,1,0:T(8,128)S(1)} %get-tuple-element.36), channel_id=1, source_target_pairs={{0,4},{1,5},{2,6},{3,7},{4,0},{5,1},{6,2},{7,3},{8,12},{9,13},{10,... | collective-permute-start | bytes 147464 | tf_op jit(solution)/shard_map/ppermute | solution.py:285
  28.2 3.5 %collective-permute-start.13 = (f32[3,32,128]{2,1,0:T(8,128)S(1)}, f32[3,32,128]{2,1,0:T(8,128)S(1)}, u32[]{:S(2)}, u32[]{:S(2)}) collective-permute-start(f32[3,32,128]{2,1,0:T(8,128)S(1)} %get-tuple-element.37), channel_id=1, source_target_pairs={{0,2},{1,3},{2,4},{3,5},{4,6},{5,7},{6,0},{7,1},{8,10},{9,11},{10,... | collective-permute-start | bytes 147464 | tf_op jit(solution)/shard_map/ppermute | solution.py:285
  31.8 2.3 %collective-permute-start.15 = (f32[3,32,128]{2,1,0:T(8,128)S(1)}, f32[3,32,128]{2,1,0:T(8,128)S(1)}, u32[]{:S(2)}, u32[]{:S(2)}) collective-permute-start(f32[3,32,128]{2,1,0:T(8,128)S(1)} %get-tuple-element.32.refs_4_), channel_id=1, source_target_pairs={{0,6},{1,7},{2,0},{3,1},{4,2},{5,3},{6,4},{7,5},{8,14},{9,15},{10,... | collective-permute-start | bytes 147464 | tf_op jit(solution)/shard_map/ppermute | solution.py:285
  32.3 4.1 %collective-permute-start.14 = (f32[3,32,128]{2,1,0:T(8,128)S(1)}, f32[3,32,128]{2,1,0:T(8,128)S(1)}, u32[]{:S(2)}, u32[]{:S(2)}) collective-permute-start(f32[3,32,128]{2,1,0:T(8,128)S(1)} %get-tuple-element.32.refs_4_), channel_id=1, source_target_pairs={{0,4},{1,5},{2,6},{3,7},{4,0},{5,1},{6,2},{7,3},{8,12},{9,13},{10,... | collective-permute-start | bytes 147464 | tf_op jit(solution)/shard_map/ppermute | solution.py:285
  36.4 9.5 %collective-permute-start.19 = (f32[3,3,32,128]{3,2,1,0:T(8,128)S(1)}, f32[3,3,32,128]{3,2,1,0:T(8,128)S(1)}, u32[]{:S(2)}, u32[]{:S(2)}) collective-permute-start(f32[3,3,32,128]{3,2,1,0:T(8,128)S(1)} %pad_maximum_fusion), channel_id=1, source_target_pairs={{0,1},{1,0},{2,3},{3,2},{4,5},{5,4},{6,7},{7,6},{8,9},{9,8},{10,11... | collective-permute-start | bytes 442376 | tf_op jit(solution)/shard_map/ppermute | solution.py:285
  37.8 4.1 %collective-permute-start.18 = (f32[3,32,128]{2,1,0:T(8,128)S(1)}, f32[3,32,128]{2,1,0:T(8,128)S(1)}, u32[]{:S(2)}, u32[]{:S(2)}) collective-permute-start(f32[3,32,128]{2,1,0:T(8,128)S(1)} %get-tuple-element.32.refs_4_), channel_id=1, source_target_pairs={{0,24},{8,0},{16,8},{24,16},{1,25},{9,1},{17,9},{25,17},{2,26},{10... | collective-permute-start | bytes 147464 | tf_op jit(solution)/shard_map/ppermute | solution.py:273
  40.0 5.0 %collective-permute-start.17 = (f32[3,32,128]{2,1,0:T(8,128)S(1)}, f32[3,32,128]{2,1,0:T(8,128)S(1)}, u32[]{:S(2)}, u32[]{:S(2)}) collective-permute-start(f32[3,32,128]{2,1,0:T(8,128)S(1)} %get-tuple-element.32.refs_4_), channel_id=1, source_target_pairs={{0,16},{8,24},{16,0},{24,8},{1,17},{9,25},{17,1},{25,9},{2,18},{10... | collective-permute-start | bytes 147464 | tf_op jit(solution)/shard_map/ppermute | solution.py:273
  40.0 5.9 %collective-permute-start.16 = (f32[3,32,128]{2,1,0:T(8,128)S(1)}, f32[3,32,128]{2,1,0:T(8,128)S(1)}, u32[]{:S(2)}, u32[]{:S(2)}) collective-permute-start(f32[3,32,128]{2,1,0:T(8,128)S(1)} %get-tuple-element.32.refs_4_), channel_id=1, source_target_pairs={{0,8},{8,16},{16,24},{24,0},{1,9},{9,17},{17,25},{25,1},{2,10},{10... | collective-permute-start | bytes 147464 | tf_op jit(solution)/shard_map/ppermute | solution.py:273
  49.3 5.3 %collective-permute-start.20 = (f32[3,3,32,128]{3,2,1,0:T(8,128)S(1)}, f32[3,3,32,128]{3,2,1,0:T(8,128)S(1)}, u32[]{:S(2)}, u32[]{:S(2)}) collective-permute-start(f32[3,3,32,128]{3,2,1,0:T(8,128)S(1)} %get-tuple-element.24), channel_id=1, source_target_pairs={{0,1},{1,0},{2,3},{3,2},{4,5},{5,4},{6,7},{7,6},{8,9},{9,8},{10,11... | collective-permute-start | bytes 442376 | tf_op jit(solution)/shard_map/ppermute | solution.py:285
  50.6 6.3 %collective-permute-start.21 = (f32[3,32,128]{2,1,0:T(8,128)S(1)}, f32[3,32,128]{2,1,0:T(8,128)S(1)}, u32[]{:S(2)}, u32[]{:S(2)}) collective-permute-start(f32[3,32,128]{2,1,0:T(8,128)S(1)} %get-tuple-element.25), channel_id=1, source_target_pairs={{0,24},{8,0},{16,8},{24,16},{1,25},{9,1},{17,9},{25,17},{2,26},{10... | collective-permute-start | bytes 147464 | tf_op jit(solution)/shard_map/ppermute | solution.py:273
  50.7 6.1 %collective-permute-start.22 = (f32[3,32,128]{2,1,0:T(8,128)S(1)}, f32[3,32,128]{2,1,0:T(8,128)S(1)}, u32[]{:S(2)}, u32[]{:S(2)}) collective-permute-start(f32[3,32,128]{2,1,0:T(8,128)S(1)} %get-tuple-element.26), channel_id=1, source_target_pairs={{0,16},{8,24},{16,0},{24,8},{1,17},{9,25},{17,1},{25,9},{2,18},{10... | collective-permute-start | bytes 147464 | tf_op jit(solution)/shard_map/ppermute | solution.py:273
  51.0 6.5 %collective-permute-start.23 = (f32[3,32,128]{2,1,0:T(8,128)S(1)}, f32[3,32,128]{2,1,0:T(8,128)S(1)}, u32[]{:S(2)}, u32[]{:S(2)}) collective-permute-start(f32[3,32,128]{2,1,0:T(8,128)S(1)} %get-tuple-element.27), channel_id=1, source_target_pairs={{0,8},{8,16},{16,24},{24,0},{1,9},{9,17},{17,25},{25,1},{2,10},{10... | collective-permute-start | bytes 147464 | tf_op jit(solution)/shard_map/ppermute | solution.py:273
  54.6 4.3 %collective-permute-start.24 = (f32[3,32,128]{2,1,0:T(8,128)S(1)}, f32[3,32,128]{2,1,0:T(8,128)S(1)}, u32[]{:S(2)}, u32[]{:S(2)}) collective-permute-start(f32[3,32,128]{2,1,0:T(8,128)S(1)} %get-tuple-element.34), channel_id=1, source_target_pairs={{0,4},{1,5},{2,6},{3,7},{4,0},{5,1},{6,2},{7,3},{8,12},{9,13},{10,... | collective-permute-start | bytes 147464 | tf_op jit(solution)/shard_map/ppermute | solution.py:285
  56.8 3.5 %collective-permute-start.25 = (f32[3,32,128]{2,1,0:T(8,128)S(1)}, f32[3,32,128]{2,1,0:T(8,128)S(1)}, u32[]{:S(2)}, u32[]{:S(2)}) collective-permute-start(f32[3,32,128]{2,1,0:T(8,128)S(1)} %get-tuple-element.35), channel_id=1, source_target_pairs={{0,2},{1,3},{2,4},{3,5},{4,6},{5,7},{6,0},{7,1},{8,10},{9,11},{10,... | collective-permute-start | bytes 147464 | tf_op jit(solution)/shard_map/ppermute | solution.py:285
where the time goes:
time: 61.2 us; the launch traced here: 61 us
  starting transfers between devices  31.1 us (51%)
  waiting for transfers between devices  20.3 us (33%)
  Pallas kernels  6.65 us (11%)
  other arithmetic  1.57 us (3%)
  between operations  1.4 us (2%)
    ppermute x14, starting transfers between devices, shift_plane(): return lax.ppermute(value, ('gy', 'gz'), pairs)  15.8 us
    ppermute x12, starting transfers between devices, shift_row(): lax.ppermute(value, 'gx', [(at, (at + steps) % count) for at in range(cou...  15.3 us
    ppermute x14, waiting for transfers between devices, shift_plane(): return lax.ppermute(value, ('gy', 'gz'), pairs)  12.1 us
    ppermute x12, waiting for transfers between devices, shift_row(): lax.ppermute(value, 'gx', [(at, (at + steps) % count) for at in range(cou...  8.18 us
    pallas_call x2, Pallas kernels, pair_forces(): pl.pallas_call(kernel, out_shape=out_shape, in_specs=[smem] * 4 + [vmem]...  6.65 us
  transfers between devices with their start and end apart: 26, of which 16 were waited for; matrix products, arithmetic and copies ran while one was open for 0% of the time, Pallas kernels for 0%

commit v1 on v0

--- a/solution.py
+++ b/solution.py
@@ -12,7 +12,7 @@
 repulsion = 4.0
 reach = 2
 lines = 3
-group = 64
+group = 128
 lead = 8
 planes = 24
 grant = 32 << 20
@@ -285,6 +285,31 @@
     return lax.ppermute(value, ("gy", "gz"), pairs)
 
 
+def swap_row(value, mask, count):
+    return lax.ppermute(value, "gx", [(at, at ^ mask) for at in range(count)])
+
+
+def swappable(rows, row_count):
+    return row_count in (2, 4) and len(rows) == row_count
+
+
+def by_offset(swapped):
+    odd = lax.axis_index("gx") % 2 == 1
+    if 3 not in swapped:
+        return dict(swapped)
+    return {
+        1: jnp.where(odd, swapped[3], swapped[1]),
+        2: swapped[2],
+        3: jnp.where(odd, swapped[1], swapped[3]),
+    }
+
+
+def fetch_row(value, offset, rows, row_count):
+    if swappable(rows, row_count):
+        return swap_row(value, offset, row_count)
+    return shift_row(value, -offset, row_count)
+
+
 def plan(row_count, line_count, height_count):
     rows_held = min(row_count, 2 * reach + 1)
     lines_held = min(line_count, lines)
@@ -293,22 +318,26 @@
     return rows, plates, lines_held
 
 
-def issue_order(rows, plates):
-    far_rows = sorted((offset for offset in rows if offset != 0), reverse=True)
+def first_order(rows, plates):
+    away = far_rows(rows)
     near = sorted((place for place in plates if place != (0, 0)), key=lambda at: (-at[1], -at[0]))
-    return far_rows + near
+    diagonal = [place for place in near if place[0] and place[1]]
+    straight = [place for place in near if not (place[0] and place[1])]
+    return away[:-1] + diagonal + away[-1:] + straight
 
 
 def collect(value, rows, plates, sizes):
     row_count, line_count, height_count = sizes
     got = {}
-    issued = issue_order(rows, plates)[::-1]
+    issued = first_order(rows, plates)[::-1]
     for place in issued:
         if isinstance(place, tuple):
             line, rise = place
             got[place] = shift_plane(value, -line, -rise, line_count, height_count)
         else:
-            got[place] = shift_row(value, -place, row_count)
+            got[place] = fetch_row(value, place, rows, row_count)
+    if swappable(rows, row_count):
+        got.update(by_offset({place: got[place] for place in far_rows(rows)}))
     got[0] = value
     operands = [0] + issued
     where = [(operands.index(key), None) for key in rows]
@@ -322,17 +351,25 @@
 
 def collect_again(value, rows, lines_held, sizes):
     row_count, line_count, height_count = sizes
+    got_lines = {0: value}
+    for line in range(lines_held - 1, 0, -1):
+        got_lines[line] = shift_plane(value, -line, 0, line_count, height_count)
+    got_rows = {}
+    for offset in far_rows(rows):
+        got_rows[offset] = fetch_row(value, offset, rows, row_count)
+    if swappable(rows, row_count):
+        got_rows = by_offset(got_rows)
+    column = jnp.stack([got_lines[line] for line in range(lines_held)])
     operands = [value]
-    where_line = [0]
+    where_line = {0: 0}
+    where_row = {0: 0}
+    where_rise = {}
     for line in range(lines_held - 1, 0, -1):
-        operands.append(shift_plane(value, -line, 0, line_count, height_count))
-    where_line += list(range(lines_held - 1, 0, -1))
-    where_row = {0: 0}
+        operands.append(got_lines[line])
+        where_line[line] = len(operands) - 1
     for offset in far_rows(rows):
-        operands.append(shift_row(value, -offset, row_count))
+        operands.append(got_rows[offset])
         where_row[offset] = len(operands) - 1
-    column = jnp.stack([operands[at] for at in where_line])
-    where_rise = {}
     for rise in range(1, height_count):
         operands.append(shift_plane(column, 0, -rise, line_count, height_count))
         where_rise[rise] = len(operands) - 1

time: 61.2 us -> 60.8 us (level)
  Pallas kernels: 6.65 us -> 10.4 us
  starting transfers between devices: 31.1 us -> 27.8 us
  waiting for transfers between devices: 20.3 us -> 18.5 us
  local copies, waits for them, and re-layouts: 0.03 us -> 0.67 us
    ppermute x12 -> x6, starting transfers between devices: 15.3 us -> 5.88 us  [shift_row(): lax.ppermute(value, 'gx', [(at, (at + steps) % count) for at in range(cou...]
    ppermute x0 -> x6, starting transfers between devices: none -> 9.35 us  [swap_row(): return lax.ppermute(value, 'gx', [(at, at ^ mask) for at in range(count)])]
    ppermute x14, waiting for transfers between devices: 12.1 us -> 6.37 us  [shift_plane(): return lax.ppermute(value, ('gy', 'gz'), pairs)]
    ppermute x0 -> x6, waiting for transfers between devices: none -> 5.53 us  [swap_row(): return lax.ppermute(value, 'gx', [(at, at ^ mask) for at in range(count)])]
    pallas_call x2, Pallas kernels: 6.65 us -> 10.4 us  [pair_forces(): pl.pallas_call(kernel, out_shape=out_shape, in_specs=[smem] * 4 + [vmem]...]
    ppermute x14, starting transfers between devices: 15.8 us -> 12.6 us  [shift_plane(): return lax.ppermute(value, ('gy', 'gz'), pairs)]
    ppermute x12 -> x6, waiting for transfers between devices: 8.18 us -> 6.65 us  [shift_row(): lax.ppermute(value, 'gx', [(at, (at + steps) % count) for at in range(cou...]
    unnamed x8, local copies, waits for them, and re-layouts: 0.02 us -> 0.67 us
  transfers between devices with their start and end apart: 26 -> 26, of which waited for: 16 -> 13; matrix products, arithmetic and copies ran while one was open for 0% -> 0% of each run, Pallas kernels for 0% -> 0%
where the time goes in v1:
time: 60.8 us; the launch traced here: 60.5 us
  starting transfers between devices  27.8 us (46%)
  waiting for transfers between devices  18.5 us (30%)
  Pallas kernels  10.4 us (17%)
  other arithmetic  1.59 us (3%)
  between operations  1.44 us (2%)
  local copies, waits for them, and re-layouts  0.67 us (1%)
    ppermute x14, starting transfers between devices, shift_plane(): return lax.ppermute(value, ('gy', 'gz'), pairs)  12.6 us
    pallas_call x2, Pallas kernels, pair_forces(): pl.pallas_call(kernel, out_shape=out_shape, in_specs=[smem] * 4 + [vmem]...  10.4 us
    ppermute x6, starting transfers between devices, swap_row(): return lax.ppermute(value, 'gx', [(at, at ^ mask) for at in range(count)])  9.35 us
    ppermute x6, waiting for transfers between devices, shift_row(): lax.ppermute(value, 'gx', [(at, (at + steps) % count) for at in range(cou...  6.65 us
    ppermute x14, waiting for transfers between devices, shift_plane(): return lax.ppermute(value, ('gy', 'gz'), pairs)  6.37 us
    ppermute x6, starting transfers between devices, shift_row(): lax.ppermute(value, 'gx', [(at, (at + steps) % count) for at in range(cou...  5.88 us
    ppermute x6, waiting for transfers between devices, swap_row(): return lax.ppermute(value, 'gx', [(at, at ^ mask) for at in range(count)])  5.53 us
  transfers between devices with their start and end apart: 26, of which 13 were waited for; matrix products, arithmetic and copies ran while one was open for 0% of the time, Pallas kernels for 0%

profile of v1, /device:TPU:0, one launch (start us, length us, event | category | flops | bytes accessed | tf_op | source)
XLA Modules:
  0.0 60.5 jit_solution(586802972325863977)
XLA Ops:
  0.6 0.8 %pad_maximum_fusion.1.refs_4_.refs_13_.refs_11_ = f32[4,32,128]{2,1,0:T(8,128)S(1)} fusion(f32[1,32,128]{2,1,0:T(8,128)} %bitcast.97, f32[3,32,128]{2,1,0:T(8,128)} %bitcast.95), kind=kLoop, calls=%fused_computation.1 | loop fusion | flops 16384 | bytes 131072 | tf_op jit(solution)/shard_map/concatenate | solution.py:425
  1.5 4.1 %collective-permute-start.7 = (f32[4,32,128]{2,1,0:T(8,128)S(1)}, f32[4,32,128]{2,1,0:T(8,128)S(1)}, u32[]{:S(2)}, u32[]{:S(2)}) collective-permute-start(f32[4,32,128]{2,1,0:T(8,128)S(1)} %pad_maximum_fusion.1.refs_4_.refs_13_.refs_11_), channel_id=1, source_target_pairs={{0,16},{8,24},{16,0},{24,8},{1,17},{9,25},{17,1},{25,9},{2,18},{10... | collective-permute-start | bytes 196616 | tf_op jit(solution)/shard_map/ppermute | solution.py:289
  5.5 2.4 %collective-permute-start.6 = (f32[4,32,128]{2,1,0:T(8,128)S(1)}, f32[4,32,128]{2,1,0:T(8,128)S(1)}, u32[]{:S(2)}, u32[]{:S(2)}) collective-permute-start(f32[4,32,128]{2,1,0:T(8,128)S(1)} %pad_maximum_fusion.1.refs_4_.refs_13_.refs_11_), channel_id=1, source_target_pairs={{0,5},{1,4},{2,7},{3,6},{4,1},{5,0},{6,3},{7,2},{8,13},{9,12},{10,... | collective-permute-start | bytes 196616 | tf_op jit(solution)/shard_map/ppermute | solution.py:285
  8.0 1.6 %collective-permute-start.4 = (f32[4,32,128]{2,1,0:T(8,128)S(1)}, f32[4,32,128]{2,1,0:T(8,128)S(1)}, u32[]{:S(2)}, u32[]{:S(2)}) collective-permute-start(f32[4,32,128]{2,1,0:T(8,128)S(1)} %pad_maximum_fusion.1.refs_4_.refs_13_.refs_11_), channel_id=1, source_target_pairs={{0,8},{8,0},{16,24},{24,16},{1,9},{9,1},{17,25},{25,17},{2,10},{10... | collective-permute-start | bytes 196616 | tf_op jit(solution)/shard_map/ppermute | solution.py:289
  10.4 0.6 %copy-done.2 = s32[1,1,1,128]{3,2,1,0:T(1,128)S(1)} copy-done((s32[1,1,1,128]{3,2,1,0:T(1,128)S(1)}, s32[1,1,1,128]{3,2,1,0:T(1,128)}, u32[]{:S(2)}) %copy-start.2) | copy-done | bytes 536
  11.2 0.9 %collective-permute-start.2 = (f32[4,32,128]{2,1,0:T(8,128)S(1)}, f32[4,32,128]{2,1,0:T(8,128)S(1)}, u32[]{:S(2)}, u32[]{:S(2)}) collective-permute-start(f32[4,32,128]{2,1,0:T(8,128)S(1)} %pad_maximum_fusion.1.refs_4_.refs_13_.refs_11_), channel_id=1, source_target_pairs={{0,1},{1,0},{2,3},{3,2},{4,5},{5,4},{6,7},{7,6},{8,9},{9,8},{10,11... | collective-permute-start | bytes 196616 | tf_op jit(solution)/shard_map/ppermute | solution.py:285
  12.6 1.0 %collective-permute-start.1 = (f32[4,32,128]{2,1,0:T(8,128)S(1)}, f32[4,32,128]{2,1,0:T(8,128)S(1)}, u32[]{:S(2)}, u32[]{:S(2)}) collective-permute-start(f32[4,32,128]{2,1,0:T(8,128)S(1)} %pad_maximum_fusion.1.refs_4_.refs_13_.refs_11_), channel_id=1, source_target_pairs={{0,4},{1,5},{2,6},{3,7},{4,0},{5,1},{6,2},{7,3},{8,12},{9,13},{10,... | collective-permute-start | bytes 196616 | tf_op jit(solution)/shard_map/ppermute | solution.py:285
  13.6 2.1 %collective-permute-done.3 = f32[4,32,128]{2,1,0:T(8,128)S(1)} collective-permute-done((f32[4,32,128]{2,1,0:T(8,128)S(1)}, f32[4,32,128]{2,1,0:T(8,128)S(1)}, u32[]{:S(2)}, u32[]{:S(2)}) %collective-permute-start.3) | collective-permute-done | bytes 65568 | tf_op jit(solution)/shard_map/ppermute | solution.py:289
  15.8 1.1 %collective-permute-done.1.refs_6_.refs_15_.refs_13_ = f32[4,32,128]{2,1,0:T(8,128)S(1)} collective-permute-done((f32[4,32,128]{2,1,0:T(8,128)S(1)}, f32[4,32,128]{2,1,0:T(8,128)S(1)}, u32[]{:S(2)}, u32[]{:S(2)}) %collective-permute-start.1) | collective-permute-done | bytes 65568 | tf_op jit(solution)/shard_map/ppermute | solution.py:285
  16.9 0.7 %collective-permute-done.refs_5_.refs_14_.refs_12_ = f32[4,32,128]{2,1,0:T(8,128)S(1)} collective-permute-done((f32[4,32,128]{2,1,0:T(8,128)S(1)}, f32[4,32,128]{2,1,0:T(8,128)S(1)}, u32[]{:S(2)}, u32[]{:S(2)}) %collective-permute-start) | collective-permute-done | bytes 65568 | tf_op jit(solution)/shard_map/ppermute | solution.py:285
  17.6 5.2 %shard_map.77 = (f32[3,32,128]{2,1,0:T(8,128)S(1)}, f32[3,32,128]{2,1,0:T(8,128)S(1)}, f32[3,32,128]{2,1,0:T(8,128)S(1)}, f32[3,32,128]{2,1,0:T(8,128)S(1)}, f32...) custom-call(s32[1]{0:T(128)} %bitcast.2.refs_0_, s32[1]{0:T(128)} %bitcast.89.refs_1_, ...), custom_call_target="tpu_custom_call" | custom-call | flops 173015040 | bytes 1048576 | tf_op jit(solution)/shard_map/pallas_call | solution.py:253
  22.8 1.5 %collective-permute-start.8 = (f32[3,3,32,128]{3,2,1,0:T(8,128)S(1)}, f32[3,3,32,128]{3,2,1,0:T(8,128)S(1)}, u32[]{:S(2)}, u32[]{:S(2)}) collective-permute-start(f32[3,3,32,128]{3,2,1,0:T(8,128)S(1)} %get-tuple-element.17), channel_id=1, source_target_pairs={{0,1},{1,0},{2,3},{3,2},{4,5},{5,4},{6,7},{7,6},{8,9},{9,8},{10,11... | collective-permute-start | bytes 442376 | tf_op jit(solution)/shard_map/ppermute | solution.py:285
  24.3 2.1 %collective-permute-start.9 = (f32[3,32,128]{2,1,0:T(8,128)S(1)}, f32[3,32,128]{2,1,0:T(8,128)S(1)}, u32[]{:S(2)}, u32[]{:S(2)}) collective-permute-start(f32[3,32,128]{2,1,0:T(8,128)S(1)} %get-tuple-element.18), channel_id=1, source_target_pairs={{0,24},{8,0},{16,8},{24,16},{1,25},{9,1},{17,9},{25,17},{2,26},{10... | collective-permute-start | bytes 147464 | tf_op jit(solution)/shard_map/ppermute | solution.py:273
  27.0 2.1 %collective-permute-done.8 = f32[3,3,32,128]{3,2,1,0:T(8,128)S(1)} collective-permute-done((f32[3,3,32,128]{3,2,1,0:T(8,128)S(1)}, f32[3,3,32,128]{3,2,1,0:T(8,128)S(1)}, u32[]{:S(2)}, u32[]{:S(2)}) %collective-permute-start.8) | collective-permute-done | bytes 147488 | tf_op jit(solution)/shard_map/ppermute | solution.py:285
  29.1 1.8 %collective-permute-start.12 = (f32[3,32,128]{2,1,0:T(8,128)S(1)}, f32[3,32,128]{2,1,0:T(8,128)S(1)}, u32[]{:S(2)}, u32[]{:S(2)}) collective-permute-start(f32[3,32,128]{2,1,0:T(8,128)S(1)} %get-tuple-element.36), channel_id=1, source_target_pairs={{0,4},{1,5},{2,6},{3,7},{4,0},{5,1},{6,2},{7,3},{8,12},{9,13},{10,... | collective-permute-start | bytes 147464 | tf_op jit(solution)/shard_map/ppermute | solution.py:285
  30.8 2.6 %collective-permute-done.10 = f32[3,32,128]{2,1,0:T(8,128)S(1)} collective-permute-done((f32[3,32,128]{2,1,0:T(8,128)S(1)}, f32[3,32,128]{2,1,0:T(8,128)S(1)}, u32[]{:S(2)}, u32[]{:S(2)}) %collective-permute-start.10) | collective-permute-done | bytes 49184 | tf_op jit(solution)/shard_map/ppermute | solution.py:273
  33.4 0.9 %collective-permute-done.13 = f32[3,32,128]{2,1,0:T(8,128)S(1)} collective-permute-done((f32[3,32,128]{2,1,0:T(8,128)S(1)}, f32[3,32,128]{2,1,0:T(8,128)S(1)}, u32[]{:S(2)}, u32[]{:S(2)}) %collective-permute-start.13) | collective-permute-done | bytes 49184 | tf_op jit(solution)/shard_map/ppermute | solution.py:285
  34.4 0.9 %collective-permute-start.14 = (f32[3,32,128]{2,1,0:T(8,128)S(1)}, f32[3,32,128]{2,1,0:T(8,128)S(1)}, u32[]{:S(2)}, u32[]{:S(2)}) collective-permute-start(f32[3,32,128]{2,1,0:T(8,128)S(1)} %get-tuple-element.32.refs_4_), channel_id=1, source_target_pairs={{0,4},{1,5},{2,6},{3,7},{4,0},{5,1},{6,2},{7,3},{8,12},{9,13},{10,... | collective-permute-start | bytes 147464 | tf_op jit(solution)/shard_map/ppermute | solution.py:285
  35.4 0.7 %collective-permute-start.18 = (f32[3,32,128]{2,1,0:T(8,128)S(1)}, f32[3,32,128]{2,1,0:T(8,128)S(1)}, u32[]{:S(2)}, u32[]{:S(2)}) collective-permute-start(f32[3,32,128]{2,1,0:T(8,128)S(1)} %get-tuple-element.32.refs_4_), channel_id=1, source_target_pairs={{0,16},{8,24},{16,0},{24,8},{1,17},{9,25},{17,1},{25,9},{2,18},{10... | collective-permute-start | bytes 147464 | tf_op jit(solution)/shard_map/ppermute | solution.py:289
  36.0 2.5 %collective-permute-start.17 = (f32[3,32,128]{2,1,0:T(8,128)S(1)}, f32[3,32,128]{2,1,0:T(8,128)S(1)}, u32[]{:S(2)}, u32[]{:S(2)}) collective-permute-start(f32[3,32,128]{2,1,0:T(8,128)S(1)} %get-tuple-element.32.refs_4_), channel_id=1, source_target_pairs={{0,24},{8,16},{16,8},{24,0},{1,25},{9,17},{17,9},{25,1},{2,26},{10... | collective-permute-start | bytes 147464 | tf_op jit(solution)/shard_map/ppermute | solution.py:289
  38.9 1.3 %collective-permute-start.19 = (f32[3,3,32,128]{3,2,1,0:T(8,128)S(1)}, f32[3,3,32,128]{3,2,1,0:T(8,128)S(1)}, u32[]{:S(2)}, u32[]{:S(2)}) collective-permute-start(f32[3,3,32,128]{3,2,1,0:T(8,128)S(1)} %pad_maximum_fusion), channel_id=1, source_target_pairs={{0,1},{1,0},{2,3},{3,2},{4,5},{5,4},{6,7},{7,6},{8,9},{9,8},{10,11... | collective-permute-start | bytes 442376 | tf_op jit(solution)/shard_map/ppermute | solution.py:285
  40.2 2.1 %collective-permute-done.17 = f32[3,32,128]{2,1,0:T(8,128)S(1)} collective-permute-done((f32[3,32,128]{2,1,0:T(8,128)S(1)}, f32[3,32,128]{2,1,0:T(8,128)S(1)}, u32[]{:S(2)}, u32[]{:S(2)}) %collective-permute-start.17) | collective-permute-done | bytes 49184 | tf_op jit(solution)/shard_map/ppermute | solution.py:289
  42.3 0.8 %collective-permute-done.16 = f32[3,32,128]{2,1,0:T(8,128)S(1)} collective-permute-done((f32[3,32,128]{2,1,0:T(8,128)S(1)}, f32[3,32,128]{2,1,0:T(8,128)S(1)}, u32[]{:S(2)}, u32[]{:S(2)}) %collective-permute-start.16) | collective-permute-done | bytes 49184 | tf_op jit(solution)/shard_map/ppermute | solution.py:289
  43.1 1.0 %collective-permute-done.19.refs_10_ = f32[3,3,32,128]{3,2,1,0:T(8,128)S(1)} collective-permute-done((f32[3,3,32,128]{3,2,1,0:T(8,128)S(1)}, f32[3,3,32,128]{3,2,1,0:T(8,128)S(1)}, u32[]{:S(2)}, u32[]{:S(2)}) %collective-permute-start.19) | collective-permute-done | bytes 147488 | tf_op jit(solution)/shard_map/ppermute | solution.py:285
  44.1 5.2 %shard_map.78 = (f32[3,32,128]{2,1,0:T(8,128)S(1)}, f32[3,32,128]{2,1,0:T(8,128)S(1)}, f32[3,32,128]{2,1,0:T(8,128)S(1)}, f32[3,32,128]{2,1,0:T(8,128)S(1)}, f32...) custom-call(s32[1]{0:T(128)} %bitcast.2.refs_0_, s32[1]{0:T(128)} %bitcast.90.refs_1_, ...), custom_call_target="tpu_custom_call" | custom-call | flops 173015040 | bytes 1048576 | tf_op jit(solution)/shard_map/pallas_call | solution.py:253
  49.3 1.4 %collective-permute-start.20 = (f32[3,3,32,128]{3,2,1,0:T(8,128)S(1)}, f32[3,3,32,128]{3,2,1,0:T(8,128)S(1)}, u32[]{:S(2)}, u32[]{:S(2)}) collective-permute-start(f32[3,3,32,128]{3,2,1,0:T(8,128)S(1)} %get-tuple-element.24), channel_id=1, source_target_pairs={{0,1},{1,0},{2,3},{3,2},{4,5},{5,4},{6,7},{7,6},{8,9},{9,8},{10,11... | collective-permute-start | bytes 442376 | tf_op jit(solution)/shard_map/ppermute | solution.py:285
  50.7 2.2 %collective-permute-start.21 = (f32[3,32,128]{2,1,0:T(8,128)S(1)}, f32[3,32,128]{2,1,0:T(8,128)S(1)}, u32[]{:S(2)}, u32[]{:S(2)}) collective-permute-start(f32[3,32,128]{2,1,0:T(8,128)S(1)} %get-tuple-element.25), channel_id=1, source_target_pairs={{0,24},{8,0},{16,8},{24,16},{1,25},{9,1},{17,9},{25,17},{2,26},{10... | collective-permute-start | bytes 147464 | tf_op jit(solution)/shard_map/ppermute | solution.py:273
  52.9 1.0 %collective-permute-start.22 = (f32[3,32,128]{2,1,0:T(8,128)S(1)}, f32[3,32,128]{2,1,0:T(8,128)S(1)}, u32[]{:S(2)}, u32[]{:S(2)}) collective-permute-start(f32[3,32,128]{2,1,0:T(8,128)S(1)} %get-tuple-element.26), channel_id=1, source_target_pairs={{0,16},{8,24},{16,0},{24,8},{1,17},{9,25},{17,1},{25,9},{2,18},{10... | collective-permute-start | bytes 147464 | tf_op jit(solution)/shard_map/ppermute | solution.py:273
  54.6 1.3 %collective-permute-start.24 = (f32[3,32,128]{2,1,0:T(8,128)S(1)}, f32[3,32,128]{2,1,0:T(8,128)S(1)}, u32[]{:S(2)}, u32[]{:S(2)}) collective-permute-start(f32[3,32,128]{2,1,0:T(8,128)S(1)} %get-tuple-element.34), channel_id=1, source_target_pairs={{0,4},{1,5},{2,6},{3,7},{4,0},{5,1},{6,2},{7,3},{8,12},{9,13},{10,... | collective-permute-start | bytes 147464 | tf_op jit(solution)/shard_map/ppermute | solution.py:285
  55.8 2.1 %collective-permute-done.22 = f32[3,32,128]{2,1,0:T(8,128)S(1)} collective-permute-done((f32[3,32,128]{2,1,0:T(8,128)S(1)}, f32[3,32,128]{2,1,0:T(8,128)S(1)}, u32[]{:S(2)}, u32[]{:S(2)}) %collective-permute-start.22) | collective-permute-done | bytes 49184 | tf_op jit(solution)/shard_map/ppermute | solution.py:273
  57.9 1.9 %collective-permute-done.23 = f32[3,32,128]{2,1,0:T(8,128)S(1)} collective-permute-done((f32[3,32,128]{2,1,0:T(8,128)S(1)}, f32[3,32,128]{2,1,0:T(8,128)S(1)}, u32[]{:S(2)}, u32[]{:S(2)}) %collective-permute-start.23) | collective-permute-done | bytes 49184 | tf_op jit(solution)/shard_map/ppermute | solution.py:273
  59.9 0.7 %add_bitcast_fusion = (f32[1,1,1,3,32,128]{5,4,3,2,1,0:T(8,128)}, f32[3,32,128]{2,1,0:T(8,128)}) fusion(f32[3,32,128]{2,1,0:T(8,128)S(1)} %get-tuple-element.32.refs_4_, f32[3,32,128]{2,1,0:T(8,128)S(1)} %get-tuple-element.33, f32[3,32,128]{2,1,0:T(8,128)S(1)} %collective-permute-done.25, f32[3,32,128]{2,1,0:T(8,128)S(1)} %collective-permute-done.24, ...), kind=kLoop, calls=%fused_computation.28 | loop fusion | flops 122880 | bytes 540672 | tf_op jit(solution)/shard_map/broadcast_in_dim | solution.py:444
  (41 shorter events, 2.5 us)
Async XLA Ops:
  1.5 9.7 %collective-permute-start.7 = (f32[4,32,128]{2,1,0:T(8,128)S(1)}, f32[4,32,128]{2,1,0:T(8,128)S(1)}, u32[]{:S(2)}, u32[]{:S(2)}) collective-permute-start(f32[4,32,128]{2,1,0:T(8,128)S(1)} %pad_maximum_fusion.1.refs_4_.refs_13_.refs_11_), channel_id=1, source_target_pairs={{0,16},{8,24},{16,0},{24,8},{1,17},{9,25},{17,1},{25,9},{2,18},{10... | collective-permute-start | bytes 196616 | tf_op jit(solution)/shard_map/ppermute | solution.py:289
  5.5 10.2 %collective-permute-start.6 = (f32[4,32,128]{2,1,0:T(8,128)S(1)}, f32[4,32,128]{2,1,0:T(8,128)S(1)}, u32[]{:S(2)}, u32[]{:S(2)}) collective-permute-start(f32[4,32,128]{2,1,0:T(8,128)S(1)} %pad_maximum_fusion.1.refs_4_.refs_13_.refs_11_), channel_id=1, source_target_pairs={{0,5},{1,4},{2,7},{3,6},{4,1},{5,0},{6,3},{7,2},{8,13},{9,12},{10,... | collective-permute-start | bytes 196616 | tf_op jit(solution)/shard_map/ppermute | solution.py:285
  8.0 7.8 %collective-permute-start.5 = (f32[4,32,128]{2,1,0:T(8,128)S(1)}, f32[4,32,128]{2,1,0:T(8,128)S(1)}, u32[]{:S(2)}, u32[]{:S(2)}) collective-permute-start(f32[4,32,128]{2,1,0:T(8,128)S(1)} %pad_maximum_fusion.1.refs_4_.refs_13_.refs_11_), channel_id=1, source_target_pairs={{0,7},{1,6},{2,1},{3,0},{4,3},{5,2},{6,5},{7,4},{8,15},{9,14},{10,... | collective-permute-start | bytes 196616 | tf_op jit(solution)/shard_map/ppermute | solution.py:285
  8.0 4.6 %collective-permute-start.4 = (f32[4,32,128]{2,1,0:T(8,128)S(1)}, f32[4,32,128]{2,1,0:T(8,128)S(1)}, u32[]{:S(2)}, u32[]{:S(2)}) collective-permute-start(f32[4,32,128]{2,1,0:T(8,128)S(1)} %pad_maximum_fusion.1.refs_4_.refs_13_.refs_11_), channel_id=1, source_target_pairs={{0,8},{8,0},{16,24},{24,16},{1,9},{9,1},{17,25},{25,17},{2,10},{10... | collective-permute-start | bytes 196616 | tf_op jit(solution)/shard_map/ppermute | solution.py:289
  9.5 6.2 %collective-permute-start.3 = (f32[4,32,128]{2,1,0:T(8,128)S(1)}, f32[4,32,128]{2,1,0:T(8,128)S(1)}, u32[]{:S(2)}, u32[]{:S(2)}) collective-permute-start(f32[4,32,128]{2,1,0:T(8,128)S(1)} %pad_maximum_fusion.1.refs_4_.refs_13_.refs_11_), channel_id=1, source_target_pairs={{0,24},{8,16},{16,8},{24,0},{1,25},{9,17},{17,9},{25,1},{2,26},{10... | collective-permute-start | bytes 196616 | tf_op jit(solution)/shard_map/ppermute | solution.py:289
  10.4 0.7 %copy-start.2 = (s32[1,1,1,128]{3,2,1,0:T(1,128)S(1)}, s32[1,1,1,128]{3,2,1,0:T(1,128)}, u32[]{:S(2)}) copy-start(s32[1,1,1,128]{3,2,1,0:T(1,128)} %param.10) | copy-start | bytes 1540
  10.4 0.7 %copy-start.3 = (s32[1,1,1,128]{3,2,1,0:T(1,128)S(1)}, s32[1,1,1,128]{3,2,1,0:T(1,128)}, u32[]{:S(2)}) copy-start(s32[1,1,1,128]{3,2,1,0:T(1,128)} %param.9) | copy-start | bytes 1540
  11.2 4.6 %collective-permute-start.2 = (f32[4,32,128]{2,1,0:T(8,128)S(1)}, f32[4,32,128]{2,1,0:T(8,128)S(1)}, u32[]{:S(2)}, u32[]{:S(2)}) collective-permute-start(f32[4,32,128]{2,1,0:T(8,128)S(1)} %pad_maximum_fusion.1.refs_4_.refs_13_.refs_11_), channel_id=1, source_target_pairs={{0,1},{1,0},{2,3},{3,2},{4,5},{5,4},{6,7},{7,6},{8,9},{9,8},{10,11... | collective-permute-start | bytes 196616 | tf_op jit(solution)/shard_map/ppermute | solution.py:285
  12.6 4.3 %collective-permute-start.1 = (f32[4,32,128]{2,1,0:T(8,128)S(1)}, f32[4,32,128]{2,1,0:T(8,128)S(1)}, u32[]{:S(2)}, u32[]{:S(2)}) collective-permute-start(f32[4,32,128]{2,1,0:T(8,128)S(1)} %pad_maximum_fusion.1.refs_4_.refs_13_.refs_11_), channel_id=1, source_target_pairs={{0,4},{1,5},{2,6},{3,7},{4,0},{5,1},{6,2},{7,3},{8,12},{9,13},{10,... | collective-permute-start | bytes 196616 | tf_op jit(solution)/shard_map/ppermute | solution.py:285
  15.7 1.9 %collective-permute-start = (f32[4,32,128]{2,1,0:T(8,128)S(1)}, f32[4,32,128]{2,1,0:T(8,128)S(1)}, u32[]{:S(2)}, u32[]{:S(2)}) collective-permute-start(f32[4,32,128]{2,1,0:T(8,128)S(1)} %pad_maximum_fusion.1.refs_4_.refs_13_.refs_11_), channel_id=1, source_target_pairs={{0,6},{1,7},{2,0},{3,1},{4,2},{5,3},{6,4},{7,5},{8,14},{9,15},{10,... | collective-permute-start | bytes 196616 | tf_op jit(solution)/shard_map/ppermute | solution.py:285
  22.8 6.2 %collective-permute-start.8 = (f32[3,3,32,128]{3,2,1,0:T(8,128)S(1)}, f32[3,3,32,128]{3,2,1,0:T(8,128)S(1)}, u32[]{:S(2)}, u32[]{:S(2)}) collective-permute-start(f32[3,3,32,128]{3,2,1,0:T(8,128)S(1)} %get-tuple-element.17), channel_id=1, source_target_pairs={{0,1},{1,0},{2,3},{3,2},{4,5},{5,4},{6,7},{7,6},{8,9},{9,8},{10,11... | collective-permute-start | bytes 442376 | tf_op jit(solution)/shard_map/ppermute | solution.py:285
  24.3 6.5 %collective-permute-start.9 = (f32[3,32,128]{2,1,0:T(8,128)S(1)}, f32[3,32,128]{2,1,0:T(8,128)S(1)}, u32[]{:S(2)}, u32[]{:S(2)}) collective-permute-start(f32[3,32,128]{2,1,0:T(8,128)S(1)} %get-tuple-element.18), channel_id=1, source_target_pairs={{0,24},{8,0},{16,8},{24,16},{1,25},{9,1},{17,9},{25,17},{2,26},{10... | collective-permute-start | bytes 147464 | tf_op jit(solution)/shard_map/ppermute | solution.py:273
  26.4 7.0 %collective-permute-start.10 = (f32[3,32,128]{2,1,0:T(8,128)S(1)}, f32[3,32,128]{2,1,0:T(8,128)S(1)}, u32[]{:S(2)}, u32[]{:S(2)}) collective-permute-start(f32[3,32,128]{2,1,0:T(8,128)S(1)} %get-tuple-element.19), channel_id=1, source_target_pairs={{0,16},{8,24},{16,0},{24,8},{1,17},{9,25},{17,1},{25,9},{2,18},{10... | collective-permute-start | bytes 147464 | tf_op jit(solution)/shard_map/ppermute | solution.py:273
  26.5 6.9 %collective-permute-start.11 = (f32[3,32,128]{2,1,0:T(8,128)S(1)}, f32[3,32,128]{2,1,0:T(8,128)S(1)}, u32[]{:S(2)}, u32[]{:S(2)}) collective-permute-start(f32[3,32,128]{2,1,0:T(8,128)S(1)} %get-tuple-element.20), channel_id=1, source_target_pairs={{0,8},{8,16},{16,24},{24,0},{1,9},{9,17},{17,25},{25,1},{2,10},{10... | collective-permute-start | bytes 147464 | tf_op jit(solution)/shard_map/ppermute | solution.py:273
  29.0 5.3 %copy-start = (f32[1,1,1,3,32,128]{5,4,3,2,1,0:T(8,128)S(1)}, f32[1,1,1,3,32,128]{5,4,3,2,1,0:T(8,128)}, u32[]{:S(2)}) copy-start(f32[1,1,1,3,32,128]{5,4,3,2,1,0:T(8,128)} %param.6) | copy-start | bytes 147460
  29.0 5.3 %copy-start.1 = (f32[1,1,1,3,32,128]{5,4,3,2,1,0:T(8,128)S(1)}, f32[1,1,1,3,32,128]{5,4,3,2,1,0:T(8,128)}, u32[]{:S(2)}) copy-start(f32[1,1,1,3,32,128]{5,4,3,2,1,0:T(8,128)} %param.7) | copy-start | bytes 147460
  29.1 4.4 %collective-permute-start.12 = (f32[3,32,128]{2,1,0:T(8,128)S(1)}, f32[3,32,128]{2,1,0:T(8,128)S(1)}, u32[]{:S(2)}, u32[]{:S(2)}) collective-permute-start(f32[3,32,128]{2,1,0:T(8,128)S(1)} %get-tuple-element.36), channel_id=1, source_target_pairs={{0,4},{1,5},{2,6},{3,7},{4,0},{5,1},{6,2},{7,3},{8,12},{9,13},{10,... | collective-permute-start | bytes 147464 | tf_op jit(solution)/shard_map/ppermute | solution.py:285
  30.8 3.5 %collective-permute-start.13 = (f32[3,32,128]{2,1,0:T(8,128)S(1)}, f32[3,32,128]{2,1,0:T(8,128)S(1)}, u32[]{:S(2)}, u32[]{:S(2)}) collective-permute-start(f32[3,32,128]{2,1,0:T(8,128)S(1)} %get-tuple-element.37), channel_id=1, source_target_pairs={{0,2},{1,3},{2,4},{3,5},{4,6},{5,7},{6,0},{7,1},{8,10},{9,11},{10,... | collective-permute-start | bytes 147464 | tf_op jit(solution)/shard_map/ppermute | solution.py:285
  34.4 4.5 %collective-permute-start.15 = (f32[3,32,128]{2,1,0:T(8,128)S(1)}, f32[3,32,128]{2,1,0:T(8,128)S(1)}, u32[]{:S(2)}, u32[]{:S(2)}) collective-permute-start(f32[3,32,128]{2,1,0:T(8,128)S(1)} %get-tuple-element.32.refs_4_), channel_id=1, source_target_pairs={{0,6},{1,7},{2,0},{3,1},{4,2},{5,3},{6,4},{7,5},{8,14},{9,15},{10,... | collective-permute-start | bytes 147464 | tf_op jit(solution)/shard_map/ppermute | solution.py:285
  34.4 4.4 %collective-permute-start.14 = (f32[3,32,128]{2,1,0:T(8,128)S(1)}, f32[3,32,128]{2,1,0:T(8,128)S(1)}, u32[]{:S(2)}, u32[]{:S(2)}) collective-permute-start(f32[3,32,128]{2,1,0:T(8,128)S(1)} %get-tuple-element.32.refs_4_), channel_id=1, source_target_pairs={{0,4},{1,5},{2,6},{3,7},{4,0},{5,1},{6,2},{7,3},{8,12},{9,13},{10,... | collective-permute-start | bytes 147464 | tf_op jit(solution)/shard_map/ppermute | solution.py:285
  35.4 7.8 %collective-permute-start.18 = (f32[3,32,128]{2,1,0:T(8,128)S(1)}, f32[3,32,128]{2,1,0:T(8,128)S(1)}, u32[]{:S(2)}, u32[]{:S(2)}) collective-permute-start(f32[3,32,128]{2,1,0:T(8,128)S(1)} %get-tuple-element.32.refs_4_), channel_id=1, source_target_pairs={{0,16},{8,24},{16,0},{24,8},{1,17},{9,25},{17,1},{25,9},{2,18},{10... | collective-permute-start | bytes 147464 | tf_op jit(solution)/shard_map/ppermute | solution.py:289
  36.0 6.3 %collective-permute-start.17 = (f32[3,32,128]{2,1,0:T(8,128)S(1)}, f32[3,32,128]{2,1,0:T(8,128)S(1)}, u32[]{:S(2)}, u32[]{:S(2)}) collective-permute-start(f32[3,32,128]{2,1,0:T(8,128)S(1)} %get-tuple-element.32.refs_4_), channel_id=1, source_target_pairs={{0,24},{8,16},{16,8},{24,0},{1,25},{9,17},{17,9},{25,1},{2,26},{10... | collective-permute-start | bytes 147464 | tf_op jit(solution)/shard_map/ppermute | solution.py:289
  38.5 4.6 %collective-permute-start.16 = (f32[3,32,128]{2,1,0:T(8,128)S(1)}, f32[3,32,128]{2,1,0:T(8,128)S(1)}, u32[]{:S(2)}, u32[]{:S(2)}) collective-permute-start(f32[3,32,128]{2,1,0:T(8,128)S(1)} %get-tuple-element.32.refs_4_), channel_id=1, source_target_pairs={{0,8},{8,0},{16,24},{24,16},{1,9},{9,1},{17,25},{25,17},{2,10},{10... | collective-permute-start | bytes 147464 | tf_op jit(solution)/shard_map/ppermute | solution.py:289
  38.9 5.2 %collective-permute-start.19 = (f32[3,3,32,128]{3,2,1,0:T(8,128)S(1)}, f32[3,3,32,128]{3,2,1,0:T(8,128)S(1)}, u32[]{:S(2)}, u32[]{:S(2)}) collective-permute-start(f32[3,3,32,128]{3,2,1,0:T(8,128)S(1)} %pad_maximum_fusion), channel_id=1, source_target_pairs={{0,1},{1,0},{2,3},{3,2},{4,5},{5,4},{6,7},{7,6},{8,9},{9,8},{10,11... | collective-permute-start | bytes 442376 | tf_op jit(solution)/shard_map/ppermute | solution.py:285
  49.3 5.2 %collective-permute-start.20 = (f32[3,3,32,128]{3,2,1,0:T(8,128)S(1)}, f32[3,3,32,128]{3,2,1,0:T(8,128)S(1)}, u32[]{:S(2)}, u32[]{:S(2)}) collective-permute-start(f32[3,3,32,128]{3,2,1,0:T(8,128)S(1)} %get-tuple-element.24), channel_id=1, source_target_pairs={{0,1},{1,0},{2,3},{3,2},{4,5},{5,4},{6,7},{7,6},{8,9},{9,8},{10,11... | collective-permute-start | bytes 442376 | tf_op jit(solution)/shard_map/ppermute | solution.py:285
  50.7 5.1 %collective-permute-start.21 = (f32[3,32,128]{2,1,0:T(8,128)S(1)}, f32[3,32,128]{2,1,0:T(8,128)S(1)}, u32[]{:S(2)}, u32[]{:S(2)}) collective-permute-start(f32[3,32,128]{2,1,0:T(8,128)S(1)} %get-tuple-element.25), channel_id=1, source_target_pairs={{0,24},{8,0},{16,8},{24,16},{1,25},{9,1},{17,9},{25,17},{2,26},{10... | collective-permute-start | bytes 147464 | tf_op jit(solution)/shard_map/ppermute | solution.py:273
  52.9 5.0 %collective-permute-start.22 = (f32[3,32,128]{2,1,0:T(8,128)S(1)}, f32[3,32,128]{2,1,0:T(8,128)S(1)}, u32[]{:S(2)}, u32[]{:S(2)}) collective-permute-start(f32[3,32,128]{2,1,0:T(8,128)S(1)} %get-tuple-element.26), channel_id=1, source_target_pairs={{0,16},{8,24},{16,0},{24,8},{1,17},{9,25},{17,1},{25,9},{2,18},{10... | collective-permute-start | bytes 147464 | tf_op jit(solution)/shard_map/ppermute | solution.py:273
  54.0 5.9 %collective-permute-start.23 = (f32[3,32,128]{2,1,0:T(8,128)S(1)}, f32[3,32,128]{2,1,0:T(8,128)S(1)}, u32[]{:S(2)}, u32[]{:S(2)}) collective-permute-start(f32[3,32,128]{2,1,0:T(8,128)S(1)} %get-tuple-element.27), channel_id=1, source_target_pairs={{0,8},{8,16},{16,24},{24,0},{1,9},{9,17},{17,25},{25,1},{2,10},{10... | collective-permute-start | bytes 147464 | tf_op jit(solution)/shard_map/ppermute | solution.py:273
  54.6 5.3 %collective-permute-start.24 = (f32[3,32,128]{2,1,0:T(8,128)S(1)}, f32[3,32,128]{2,1,0:T(8,128)S(1)}, u32[]{:S(2)}, u32[]{:S(2)}) collective-permute-start(f32[3,32,128]{2,1,0:T(8,128)S(1)} %get-tuple-element.34), channel_id=1, source_target_pairs={{0,4},{1,5},{2,6},{3,7},{4,0},{5,1},{6,2},{7,3},{8,12},{9,13},{10,... | collective-permute-start | bytes 147464 | tf_op jit(solution)/shard_map/ppermute | solution.py:285
  55.8 4.1 %collective-permute-start.25 = (f32[3,32,128]{2,1,0:T(8,128)S(1)}, f32[3,32,128]{2,1,0:T(8,128)S(1)}, u32[]{:S(2)}, u32[]{:S(2)}) collective-permute-start(f32[3,32,128]{2,1,0:T(8,128)S(1)} %get-tuple-element.35), channel_id=1, source_target_pairs={{0,2},{1,3},{2,4},{3,5},{4,6},{5,7},{6,0},{7,1},{8,10},{9,11},{10,... | collective-permute-start | bytes 147464 | tf_op jit(solution)/shard_map/ppermute | solution.py:285
